TPU v7x, 32 devices: a whole 2x2x4 slice. The times are simulated.
32 devices in a mesh: dp: 4 (over y, x), vocab: 8 (over z, core).
Axes of the slice: x: 2, y: 2, z: 4, core: 2. Of those that a mesh axis runs over, the one named last changes fastest.
Arguments:
- token_ids: int32 [64, 512], P(('dp', 'vocab')), may hold values from 0 to 30719, as said below
- type_ids: int32 [64, 512], P(('dp', 'vocab')), may hold values from 0 to 1
- lengths: int32 [64], P(('dp', 'vocab')), may hold values from 20 to 512, as said below
- word_table: bfloat16 [30720, 768], P('vocab'), may hold values from -6 to 6
- pos_table: bfloat16 [512, 768], replicated, may hold values from -4 to 4
- token_type_embeddings: bfloat16 [2, 768], replicated, may hold values from -4 to 4
- emb_gain: float32 [768], replicated, may hold values from 0.25 to 1.75
- emb_bias: float32 [768], replicated, may hold values from -3 to 3
- query_weight: bfloat16 [768, 768], replicated, may hold values from -0.21875 to 0.21875
- query_bias: float32 [768], replicated, may hold values from -3 to 3
- key_weight: bfloat16 [768, 768], replicated, may hold values from -0.21875 to 0.21875
- value_weight: bfloat16 [768, 768], replicated, may hold values from -0.21875 to 0.21875
- value_bias: float32 [768], replicated, may hold values from -3 to 3
- out_weight: bfloat16 [768, 768], replicated, may hold values from -0.875 to 0.875
- out_bias: float32 [768], replicated, may hold values from -3 to 3
- attn_gain: float32 [768], replicated, may hold values from 0.25 to 1.75
- attn_bias: float32 [768], replicated, may hold values from -3 to 3
- up_weight: bfloat16 [768, 3072], replicated, may hold values from -0.21875 to 0.21875
- up_bias: float32 [3072], replicated, may hold values from -3 to 3
- down_weight: bfloat16 [3072, 768], replicated, may hold values from -0.109375 to 0.109375
- down_bias: float32 [768], replicated, may hold values from -3 to 3
- final_gain: float32 [768], replicated, may hold values from 0.25 to 1.75
- final_bias: float32 [768], replicated, may hold values from -3 to 3
- cotangent: bfloat16 [64, 512, 768], P(('dp', 'vocab')), may hold values from -6 to 6
Outputs:
- encoded: float32 [64, 512, 768], P(('dp', 'vocab'))
- word_grad: float32 [30720, 768], P('vocab')
- pos_grad: float32 [512, 768], P('vocab')
- type_grad: float32 [2, 768], P(None, 'vocab')
- emb_gain_grad: float32 [768], P('vocab')
- emb_bias_grad: float32 [768], P('vocab')
- query_weight_grad: float32 [768, 768], P('vocab')
- query_bias_grad: float32 [768], P('vocab')
- key_weight_grad: float32 [768, 768], P('vocab')
- value_weight_grad: float32 [768, 768], P('vocab')
- value_bias_grad: float32 [768], P('vocab')
- out_weight_grad: float32 [768, 768], P('vocab')
- out_bias_grad: float32 [768], P('vocab')
- attn_gain_grad: float32 [768], P('vocab')
- attn_bias_grad: float32 [768], P('vocab')
- up_weight_grad: float32 [768, 3072], P('vocab')
- up_bias_grad: float32 [3072], P('vocab')
- down_weight_grad: float32 [3072, 768], P('vocab')
- down_bias_grad: float32 [768], P('vocab')
- final_gain_grad: float32 [768], P('vocab')
- final_bias_grad: float32 [768], P('vocab')
Inputs may be any that keep to these rules, and one draw needn't show every extreme that they name: `token_ids`: among the tokens of one device, at most 256 ids fall into the 3840 rows of word_table that one index of vocab holds; for one such block of rows, the same on every device, exactly 256 do. `lengths`: the tokens at positions from a sequence's length on are padding; some sequence has length 512 and some 20.
All inputs are finite; a program needn't handle non-finite values.
Results may differ from a plain program's by a relative error of at most 0.017.
Values may be sent and summed in bfloat16 or wider, within the bound.
A program may use at most 192 MiB of HBM per device.

v0:
```python
from functools import partial
import jax
import jax.numpy as jnp
from jax import lax
from jax.sharding import PartitionSpec as P

HEADS = 12
HEAD = 64
L = 512
EPSILON = 1e-12


def layer_norm(values, gain, bias):
    center = values - jnp.mean(values, -1, keepdims=True)
    spread = jnp.mean(center * center, -1, keepdims=True)
    return center * lax.rsqrt(spread + EPSILON) * gain + bias


def matmul(left, right):
    return jnp.dot(left, right, preferred_element_type=jnp.float32)


def matmul_tn(left, right):
    return lax.dot_general(
        left, right, (((0,), (0,)), ((), ())), preferred_element_type=jnp.float32
    )


def matmul_nt(left, right):
    return lax.dot_general(
        left, right, (((1,), (1,)), ((), ())), preferred_element_type=jnp.float32
    )


def masked_scores(query, keys, length):
    scores = jnp.einsum("qhd,khd->hqk", query, keys, preferred_element_type=jnp.float32) * HEAD ** (
        -0.5
    )
    visible = jnp.arange(L) < length
    return jnp.where(visible[None, None, :], scores, -1000000000.0)


def attend_forward(block):
    query, keys, values, length = block
    scores = masked_scores(query, keys, length)
    highest = jnp.max(scores, -1, keepdims=True)
    expd = jnp.exp(scores - highest)
    totals = jnp.sum(expd, -1, keepdims=True)
    probs_low = (expd / totals).astype(jnp.bfloat16)
    mixed = jnp.einsum("hqk,khd->qhd", probs_low, values, preferred_element_type=jnp.float32)
    return (mixed.astype(jnp.bfloat16), highest + jnp.log(totals))


def attend_backward(block):
    query, keys, values, grad_mixed, logsum, length = block
    probs = jnp.exp(masked_scores(query, keys, length) - logsum)
    probs_low = probs.astype(jnp.bfloat16)
    grad_values = jnp.einsum(
        "hqk,qhd->khd", probs_low, grad_mixed, preferred_element_type=jnp.float32
    )
    grad_probs = jnp.einsum("qhd,khd->hqk", grad_mixed, values, preferred_element_type=jnp.float32)
    inner = jnp.sum(grad_probs * probs, -1, keepdims=True)
    grad_scores = (probs * (grad_probs - inner)).astype(jnp.bfloat16)
    scale = HEAD ** (-0.5)
    grad_query = (
        jnp.einsum("hqk,khd->qhd", grad_scores, keys, preferred_element_type=jnp.float32) * scale
    )
    grad_keys = (
        jnp.einsum("hqk,qhd->khd", grad_scores, query, preferred_element_type=jnp.float32) * scale
    )
    return (grad_query, grad_keys, grad_values)


def local(
    token_ids,
    type_ids,
    lengths,
    word_table,
    pos_table,
    token_type_embeddings,
    emb_gain,
    emb_bias,
    query_weight,
    query_bias,
    key_weight,
    value_weight,
    value_bias,
    out_weight,
    out_bias,
    attn_gain,
    attn_bias,
    up_weight,
    up_bias,
    down_weight,
    down_bias,
    final_gain,
    final_bias,
    cotangent,
):
    seq_count, seq_len = token_ids.shape
    tokens = seq_count * seq_len
    width = word_table.shape[1]
    rows_local = word_table.shape[0]
    owners = lax.axis_size("vocab")
    capacity = max(2, 2 * tokens // owners)
    flat_ids = token_ids.reshape(tokens)
    owner = flat_ids // rows_local
    member = (owner[:, None] == jnp.arange(owners)[None, :]).astype(jnp.int32)
    earlier = jnp.cumsum(member, 0) - member
    rank = jnp.sum(earlier * member, 1)
    slot = owner * capacity + rank
    requests = (
        jnp.full((owners * capacity,), -1, jnp.int32).at[slot].set(flat_ids - owner * rows_local)
    )
    requests = requests.reshape(owners, capacity)
    asked = lax.all_to_all(requests, "vocab", split_axis=0, concat_axis=0, tiled=True)
    valid = asked >= 0
    found = word_table[jnp.maximum(asked, 0)]
    found = jnp.where(valid[..., None], found, jnp.zeros((), jnp.bfloat16))
    returned = lax.all_to_all(found, "vocab", split_axis=0, concat_axis=0, tiled=True)
    word_rows = returned.reshape(owners * capacity, width)[slot]
    kinds = token_type_embeddings.shape[0]
    selection_matrix = (type_ids[..., None] == jnp.arange(kinds)[None, None, :]).astype(jnp.float32)
    type_rows = jnp.einsum(
        "tcr,rb->tcb",
        selection_matrix,
        token_type_embeddings.astype(jnp.float32),
        precision=lax.Precision.HIGHEST,
    )
    embedded = (
        word_rows.reshape(seq_count, seq_len, width).astype(jnp.float32)
        + pos_table.astype(jnp.float32)[None]
        + type_rows
    )
    normed = layer_norm(embedded, emb_gain, emb_bias).reshape(tokens, width)
    normed_low = normed.astype(jnp.bfloat16)
    query = (matmul(normed_low, query_weight) + query_bias).astype(jnp.bfloat16)
    keys = matmul(normed_low, key_weight).astype(jnp.bfloat16)
    values = (matmul(normed_low, value_weight) + value_bias).astype(jnp.bfloat16)
    split_shape = (seq_count, seq_len, HEADS, HEAD)
    query_split = query.reshape(split_shape)
    keys_split = keys.reshape(split_shape)
    values_split = values.reshape(split_shape)
    mixed, logsum = lax.map(attend_forward, (query_split, keys_split, values_split, lengths))
    mixed_low = mixed.reshape(tokens, width)
    first = normed + matmul(mixed_low, out_weight) + out_bias
    hidden = layer_norm(first, attn_gain, attn_bias)
    hidden_reduced_precision = hidden.astype(jnp.bfloat16)
    upper = matmul(hidden_reduced_precision, up_weight) + up_bias
    active_low = jax.nn.gelu(upper, approximate=False).astype(jnp.bfloat16)
    second = hidden + matmul(active_low, down_weight) + down_bias
    encoded = layer_norm(second, final_gain, final_bias)
    grad_out = cotangent.reshape(tokens, width).astype(jnp.float32)
    _, final_pull = jax.vjp(layer_norm, second, final_gain, final_bias)
    grad_second, grad_final_gain, grad_final_bias = final_pull(grad_out)
    grad_down_bias = jnp.sum(grad_second, 0)
    second_matmul_gradient_reduced = grad_second.astype(jnp.bfloat16)
    grad_down = matmul_tn(active_low, second_matmul_gradient_reduced)
    grad_active = matmul_nt(second_matmul_gradient_reduced, down_weight)
    _, gelu_pull = jax.vjp(partial(jax.nn.gelu, approximate=False), upper)
    (grad_upper,) = gelu_pull(grad_active)
    grad_up_bias = jnp.sum(grad_upper, 0)
    grad_upper_low = grad_upper.astype(jnp.bfloat16)
    grad_up = matmul_tn(hidden_reduced_precision, grad_upper_low)
    grad_hidden = grad_second + matmul_nt(grad_upper_low, up_weight)
    _, attn_pull = jax.vjp(layer_norm, first, attn_gain, attn_bias)
    grad_first, grad_attn_gain, grad_attn_bias = attn_pull(grad_hidden)
    grad_out_bias = jnp.sum(grad_first, 0)
    grad_first_low = grad_first.astype(jnp.bfloat16)
    grad_out_weight = matmul_tn(mixed_low, grad_first_low)
    grad_mixed = matmul_nt(grad_first_low, out_weight).astype(jnp.bfloat16)
    grad_query, grad_keys, grad_values = lax.map(
        attend_backward,
        (query_split, keys_split, values_split, grad_mixed.reshape(split_shape), logsum, lengths),
    )
    grad_query = grad_query.reshape(tokens, width)
    grad_keys = grad_keys.reshape(tokens, width)
    grad_values = grad_values.reshape(tokens, width)
    grad_query_bias = jnp.sum(grad_query, 0)
    grad_value_bias = jnp.sum(grad_values, 0)
    grad_query_low = grad_query.astype(jnp.bfloat16)
    grad_keys_low = grad_keys.astype(jnp.bfloat16)
    grad_values_low = grad_values.astype(jnp.bfloat16)
    grad_query_weight = matmul_tn(normed_low, grad_query_low)
    grad_key_weight = matmul_tn(normed_low, grad_keys_low)
    grad_value_weight = matmul_tn(normed_low, grad_values_low)
    grad_normed = (
        grad_first
        + matmul_nt(grad_query_low, query_weight)
        + matmul_nt(grad_keys_low, key_weight)
        + matmul_nt(grad_values_low, value_weight)
    )
    _, emb_pull = jax.vjp(layer_norm, embedded, emb_gain, emb_bias)
    embedding_output_gradient, grad_emb_gain, grad_emb_bias = emb_pull(
        grad_normed.reshape(seq_count, seq_len, width)
    )
    grad_pos = jnp.sum(embedding_output_gradient, 0)
    token_type_gradient = jnp.einsum(
        "nox,noh->xh", selection_matrix, embedding_output_gradient, precision=lax.Precision.HIGHEST
    )
    outgoing = (
        jnp.zeros((owners * capacity, width), jnp.float32)
        .at[slot]
        .set(embedding_output_gradient.reshape(tokens, width))
    )
    incoming = lax.all_to_all(
        outgoing.reshape(owners, capacity, width).astype(jnp.bfloat16),
        "vocab",
        split_axis=0,
        concat_axis=0,
        tiled=True,
    ).astype(jnp.float32)
    keep_rows = asked >= 0
    incoming = jnp.where(keep_rows[..., None], incoming, 0.0)
    grad_word = (
        jnp.zeros((rows_local, width), jnp.float32)
        .at[jnp.maximum(asked, 0).reshape(-1)]
        .add(incoming.reshape(owners * capacity, width))
    )
    (
        grad_query_weight,
        grad_query_bias,
        grad_key_weight,
        grad_value_weight,
        grad_value_bias,
        grad_out_weight,
        grad_out_bias,
        grad_attn_gain,
        grad_attn_bias,
        grad_emb_gain,
        grad_emb_bias,
        grad_pos,
        token_type_gradient,
        grad_down,
        grad_down_bias,
        grad_up,
        grad_up_bias,
        grad_final_gain,
        grad_final_bias,
    ) = (
        lax.psum_scatter(grad_query_weight, "vocab", scatter_dimension=0, tiled=True),
        lax.psum_scatter(grad_query_bias, "vocab", scatter_dimension=0, tiled=True),
        lax.psum_scatter(grad_key_weight, "vocab", scatter_dimension=0, tiled=True),
        lax.psum_scatter(grad_value_weight, "vocab", scatter_dimension=0, tiled=True),
        lax.psum_scatter(grad_value_bias, "vocab", scatter_dimension=0, tiled=True),
        lax.psum_scatter(grad_out_weight, "vocab", scatter_dimension=0, tiled=True),
        lax.psum_scatter(grad_out_bias, "vocab", scatter_dimension=0, tiled=True),
        lax.psum_scatter(grad_attn_gain, "vocab", scatter_dimension=0, tiled=True),
        lax.psum_scatter(grad_attn_bias, "vocab", scatter_dimension=0, tiled=True),
        lax.psum_scatter(grad_emb_gain, "vocab", scatter_dimension=0, tiled=True),
        lax.psum_scatter(grad_emb_bias, "vocab", scatter_dimension=0, tiled=True),
        lax.psum_scatter(grad_pos, "vocab", scatter_dimension=0, tiled=True),
        lax.psum_scatter(token_type_gradient, "vocab", scatter_dimension=1, tiled=True),
        lax.psum_scatter(grad_down, "vocab", scatter_dimension=0, tiled=True),
        lax.psum_scatter(grad_down_bias, "vocab", scatter_dimension=0, tiled=True),
        lax.psum_scatter(grad_up, "vocab", scatter_dimension=0, tiled=True),
        lax.psum_scatter(grad_up_bias, "vocab", scatter_dimension=0, tiled=True),
        lax.psum_scatter(grad_final_gain, "vocab", scatter_dimension=0, tiled=True),
        lax.psum_scatter(grad_final_bias, "vocab", scatter_dimension=0, tiled=True),
    )
    (
        grad_query_weight,
        grad_query_bias,
        grad_key_weight,
        grad_value_weight,
        grad_value_bias,
        grad_out_weight,
        grad_out_bias,
        grad_attn_gain,
        grad_attn_bias,
        grad_emb_gain,
        grad_emb_bias,
        grad_pos,
        token_type_gradient,
        grad_down,
        grad_down_bias,
        grad_up,
        grad_up_bias,
        grad_final_gain,
        grad_final_bias,
        grad_word,
    ) = (
        lax.psum(grad_query_weight.astype(jnp.bfloat16), "dp").astype(jnp.float32),
        lax.psum(grad_query_bias.astype(jnp.bfloat16), "dp").astype(jnp.float32),
        lax.psum(grad_key_weight.astype(jnp.bfloat16), "dp").astype(jnp.float32),
        lax.psum(grad_value_weight.astype(jnp.bfloat16), "dp").astype(jnp.float32),
        lax.psum(grad_value_bias.astype(jnp.bfloat16), "dp").astype(jnp.float32),
        lax.psum(grad_out_weight.astype(jnp.bfloat16), "dp").astype(jnp.float32),
        lax.psum(grad_out_bias.astype(jnp.bfloat16), "dp").astype(jnp.float32),
        lax.psum(grad_attn_gain.astype(jnp.bfloat16), "dp").astype(jnp.float32),
        lax.psum(grad_attn_bias.astype(jnp.bfloat16), "dp").astype(jnp.float32),
        lax.psum(grad_emb_gain.astype(jnp.bfloat16), "dp").astype(jnp.float32),
        lax.psum(grad_emb_bias.astype(jnp.bfloat16), "dp").astype(jnp.float32),
        lax.psum(grad_pos.astype(jnp.bfloat16), "dp").astype(jnp.float32),
        lax.psum(token_type_gradient.astype(jnp.bfloat16), "dp").astype(jnp.float32),
        lax.psum(grad_down.astype(jnp.bfloat16), "dp").astype(jnp.float32),
        lax.psum(grad_down_bias.astype(jnp.bfloat16), "dp").astype(jnp.float32),
        lax.psum(grad_up.astype(jnp.bfloat16), "dp").astype(jnp.float32),
        lax.psum(grad_up_bias.astype(jnp.bfloat16), "dp").astype(jnp.float32),
        lax.psum(grad_final_gain.astype(jnp.bfloat16), "dp").astype(jnp.float32),
        lax.psum(grad_final_bias.astype(jnp.bfloat16), "dp").astype(jnp.float32),
        lax.psum(grad_word.astype(jnp.bfloat16), "dp").astype(jnp.float32),
    )
    return (
        encoded.reshape(seq_count, seq_len, width),
        grad_word,
        grad_pos,
        token_type_gradient,
        grad_emb_gain,
        grad_emb_bias,
        grad_query_weight,
        grad_query_bias,
        grad_key_weight,
        grad_value_weight,
        grad_value_bias,
        grad_out_weight,
        grad_out_bias,
        grad_attn_gain,
        grad_attn_bias,
        grad_up,
        grad_up_bias,
        grad_down,
        grad_down_bias,
        grad_final_gain,
        grad_final_bias,
    )


def solution(mesh):
    placed = (
        P(("dp", "vocab"), None),
        P(("dp", "vocab"), None),
        P(("dp", "vocab")),
        P("vocab", None),
        P(),
        P(),
        P(),
        P(),
        P(),
        P(),
        P(),
        P(),
        P(),
        P(),
        P(),
        P(),
        P(),
        P(),
        P(),
        P(),
        P(),
        P(),
        P(),
        P(("dp", "vocab"), None, None),
    )
    return jax.shard_map(
        local,
        mesh=mesh,
        in_specs=placed,
        out_specs=(
            P(("dp", "vocab"), None, None),
            P("vocab", None),
            P("vocab", None),
            P(None, "vocab"),
            P("vocab"),
            P("vocab"),
            P("vocab", None),
            P("vocab"),
            P("vocab", None),
            P("vocab", None),
            P("vocab"),
            P("vocab", None),
            P("vocab"),
            P("vocab"),
            P("vocab"),
            P("vocab", None),
            P("vocab"),
            P("vocab", None),
            P("vocab"),
            P("vocab"),
            P("vocab"),
        ),
        check_vma=False,
    )
```

profile of v0, /device:TPU:0, one launch (start us, length us, event | category | flops | bytes accessed | tf_op | source)
XLA Modules:
  0.0 1033.5 jit_solution(1598047318248244611)
XLA Ops:
  13.7 4.3 scatter_custom_fusion
  18.1 11.7 %all_to_all.19 = s32[8,1,256]{2,1,0:T(1,128)S(1)} all-to-all(s32[8,1,256]{2,1,0:T(1,128)S(1)} %bitcast.272), channel_id=1, replica_groups=mesh['dp'=4,'vocab'=8] {'vocab'}, dimensions={0} | all-to-all | bytes 16384 | tf_op jit(solution)/shard_map/all_to_all | solution.py:116
  30.4 13.5 %gather_fusion = bf16[2048,768]{1,0:T(8,128)(2,1)} fusion(bf16[3840,768]{1,0:T(8,128)(2,1)} %param.31, s32[2048]{0:T(1024)S(1)} %broadcast_clamp_fusion), kind=kCustom, calls=%fused_computation | custom fusion | bytes 6299648 | tf_op jit(solution)/shard_map/gather | solution.py:118
  47.8 4.6 all-to-all-start.1
  52.8 71.1 %all-to-all-done.1 = bf16[8,256,768]{2,1,0:T(8,128)(2,1)} async-done(((bf16[8,256,768]{2,1,0:T(8,128)(2,1)}), bf16[8,256,768]{2,1,0:T(8,128)(2,1)}, u32[]{:S(2)}, u32[]{:S(2)}) %all-to-all-start.1) | async-done | bytes 3145760 | tf_op jit(solution)/shard_map/all_to_all | solution.py:120
  123.9 7.9 gather_fusion.1
  167.7 25.7 %while.26 = (s32[]{:T(128)}, bf16[2,512,12,64]{1,3,2,0:T(8,128)(2,1)}, f32[2,12,512,1]{2,1,3,0:T(8,128)}, bf16[2,512,12,64]{1,3,2,0:T(8,128)(2,1)}, s32[2]{0:T(1...) while((s32[]{:T(128)}, ...), condition=%wide.region_9.10_spmd, body=%wide.region_6.9_spmd.sunk | while | flops 843442688 | bytes 47411340 | solution.py:144
  169.2 4.1 fusion.155
  175.9 4.2 fusion.157
  181.9 4.1 fusion.155
  188.6 4.2 fusion.157
  193.4 3.6 copy.106
  201.9 35.5 %multiply_convert_fusion.1 = (bf16[1024,3072]{1,0:T(8,128)(2,1)S(1)}, f32[1024,3072]{1,0:T(8,128)}, f32[1024,3072]{1,0:T(8,128)}) fusion(f32[3072]{0:T(1024)S(1)} %copy-done.74, bf16[768,3072]{1,0:T(8,128)(2,1)S(1)} %bitcast.284, f32[1024,768]{1,0:T(8,128)S(1)} %get-tuple-element.280, f32[768]{0:T(1024)S(1)} %copy-done.48, f32[768]{0:T(1024)S(1)} %copy-done.42, ...), kind=kOutput, calls=%fused_computation.64 | convolution fusion | flops 5043388416 | bytes 39348224 | tf_op jit(solution)/shard_map/dot_general | solution.py:20
  237.5 5.4 fusion.98
  246.1 3.5 fusion.92
  249.6 19.6 %fusion.100 = (f32[3072]{0:T(1024)}, bf16[1024,3072]{1,0:T(8,128)(2,1)}) fusion(f32[1024,3072]{1,0:T(8,128)} %get-tuple-element.265, bf16[3072,768]{1,0:T(8,128)(2,1)} %param.47, f32[1024,768]{1,0:T(8,128)} %get-tuple-element.263, f32[1024]{0:T(1024)S(1)} %negate_multiply_fusion.3, f32[1024,3072]{1,0:T(8,128)} %get-tuple-element.281, f32[3072]{0:T(1024)S(1)} %copy-done.74), kind=kOutput, calls=%fused_computation.197 | convolution fusion | flops 4883739648 | bytes 39350272 | tf_op jit(solution)/shard_map/dot_general | solution.py:30
  269.2 11.6 %multiply_reduce_fusion.1 = (f32[768]{0:T(1024)}, f32[1024]{0:T(1024)S(1)}, f32[768]{0:T(1024)}, f32[1024,768]{1,0:T(8,128)S(1)}) fusion(f32[1024,768]{1,0:T(8,128)} %copy-done.7, f32[1024]{0:T(1024)S(1)} %fusion.81, f32[1024]{0:T(1024)S(1)} %broadcast_multiply_fusion.1, f32[768]{0:T(1024)S(1)} %copy-done.42, bf16[768,3072]{1,0:T(8,128)(2,1)} %param.45, ...), kind=kOutput, calls=%fused_computation.96 | convolution fusion | flops 4839699456 | bytes 20472832 | tf_op jit(solution)/shard_map/dot_general | solution.py:30
  287.1 4.0 reshape.389
  294.0 55.2 %while.27 = (s32[]{:T(128)}, f32[2,512,12,64]{1,3,2,0:T(8,128)}, bf16[2,512,12,64]{1,3,2,0:T(8,128)(2,1)}, f32[2,512,12,64]{1,3,2,0:T(8,128)}, bf16[2,512,12,64]...) while((s32[]{:T(128)}, f32[2,512,12,64]{1,3,2,0:T(8,128)}, ...), condition=%wide.region_20.21_spmd, body=%wide.region_18.20_spmd.sunk | while | flops 2061232640 | bytes 186580400 | solution.py:172
  301.6 7.3 multiply_reduce_fusion.9
  309.0 7.2 multiply_convert_fusion.3
  328.9 7.3 multiply_reduce_fusion.9
  336.3 7.2 multiply_convert_fusion.3
  349.1 5.5 fusion.94
  371.4 3.4 reduce_sum.274
  374.9 5.3 fusion.86
  380.3 4.7 fusion.104
  385.1 4.8 fusion.103
  389.9 4.2 fusion.105
  394.2 10.7 %fusion.85 = f32[3072,768]{1,0:T(8,128)} fusion(bf16[1024,3072]{1,0:T(8,128)(2,1)} %copy-done.82, f32[1024,768]{1,0:T(8,128)} %get-tuple-element.263, f32[1024]{0:T(1024)S(1)} %copy-done.58), kind=kOutput, calls=%fused_computation.185 | convolution fusion | flops 4833411072 | bytes 18878464 | tf_op jit(solution)/shard_map/dot_general | solution.py:24
  405.6 11.3 %fusion.60 = f32[768,3072]{1,0:T(8,128)} fusion(bf16[1024,3072]{1,0:T(8,128)(2,1)} %get-tuple-element.288, f32[1024,768]{1,0:T(8,128)} %copy-done.7, f32[768]{0:T(1024)S(1)} %copy-done.49, f32[768]{0:T(1024)S(1)} %copy-done.43, f32[1024]{0:T(1024)S(1)} %copy-done.39, f32[1024]{0:T(1024)S(1)} %copy-done.37), kind=kOutput, calls=%fused_computation.101 | convolution fusion | flops 4835770368 | bytes 18888704 | tf_op jit(solution)/shard_map/dot_general | solution.py:24
  416.9 8.7 scatter_custom_fusion.1
  425.6 4.8 convert_element_type.252
  430.4 4.6 all-to-all-start.2
  435.1 5.3 convolution_bitcast_fusion
  442.1 5.9 reduce-scatter.19.cloned.1.call-done
  449.6 70.5 %reduce-scatter.15.cloned.1.call-done = f32[96,768]{1,0:T(8,128)} async-done(((f32[768,768]{1,0:T(8,128)}), f32[96,768]{1,0:T(8,128)}) %reduce-scatter.15.cloned.1.call-update) | async-done | bytes 294928 | tf_op jit(solution)/shard_map/reduce_scatter | solution.py:243
  521.7 44.2 %reduce-scatter.13.cloned.1.call-done = f32[96,768]{1,0:T(8,128)} async-done(((f32[768,768]{1,0:T(8,128)}), f32[96,768]{1,0:T(8,128)}) %reduce-scatter.13.cloned.1.call-update) | async-done | bytes 294928 | tf_op jit(solution)/shard_map/reduce_scatter | solution.py:241
  567.6 36.2 %reduce-scatter.17.cloned.1.call-done = f32[96,768]{1,0:T(8,128)} async-done(((f32[768,768]{1,0:T(8,128)}), f32[96,768]{1,0:T(8,128)}) %reduce-scatter.17.cloned.1.call-update) | async-done | bytes 294928 | tf_op jit(solution)/shard_map/reduce_scatter | solution.py:244
  605.5 4.6 convert_select_fusion
  610.1 20.6 %scatter_custom_fusion.2 = f32[3840,768]{1,0:T(8,128)} fusion(s32[2048]{0:T(1024)} %bitcast.271, f32[2048,768]{1,0:T(8,128)} %bitcast.250, f32[]{:T(128)} %constant.47.clone.1), kind=kCustom, calls=%fused_computation.79 | custom fusion | flops 1572864 | bytes 11796992 | tf_op jit(solution)/shard_map/scatter-add | solution.py:218
  630.7 7.5 convert_element_type.255
  638.2 66.6 %reduce-scatter.23.cloned.1.call-done = f32[384,768]{1,0:T(8,128)} async-done(((f32[3072,768]{1,0:T(8,128)}), f32[384,768]{1,0:T(8,128)}) %reduce-scatter.23.cloned.1.call-update) | async-done | bytes 1179664 | tf_op jit(solution)/shard_map/reduce_scatter | solution.py:254
  706.9 98.1 %reduce-scatter.21.cloned.1.call-done = f32[96,3072]{1,0:T(8,128)} async-done(((f32[768,3072]{1,0:T(8,128)}), f32[96,3072]{1,0:T(8,128)}) %reduce-scatter.21.cloned.1.call-update) | async-done | bytes 1179664 | tf_op jit(solution)/shard_map/reduce_scatter | solution.py:256
  814.6 26.7 %all-reduce.11 = (bf16[768]{0:T(1024)(128)(2,1)S(1)}, bf16[768]{0:T(1024)(128)(2,1)S(1)}, bf16[768]{0:T(1024)(128)(2,1)S(1)}, bf16[768]{0:T(1024)(128)(2,1)S(1)}...) all-reduce(f32[768]{0:T(1024)S(1)} %get-tuple-element.190, ...), channel_id=4, replica_groups=mesh['dp'=4,'vocab'=8] {'vocab'}, use_global_device_ids=true, to_apply=%region_32.33.clone | all-reduce | flops 10752 | bytes 64512
  843.0 10.2 all-reduce.12
  859.5 147.5 %all-reduce.16.cloned.1.call-done = (bf16[3840,768]{1,0:T(8,128)(2,1)}, bf16[64,768]{1,0:T(8,128)(2,1)}, bf16[96,768]{1,0:T(8,128)(2,1)}, bf16[96,768]{1,0:T(8,1...) async-done(((bf16[3840,768]{1,0:T(8,128)(2,1)}, bf16[64,768]{1,0:T(8,128)(2,1)}, ...) | async-done | bytes 7766032 | tf_op jit(solution)/shard_map/psum | solution.py:302
  1018.5 8.2 convert_element_type.256
  (362 shorter events, 153.8 us)
Async XLA Ops:
  7.2 190.3 %copy-start = (bf16[768,768]{1,0:T(8,128)(2,1)S(1)}, bf16[768,768]{1,0:T(8,128)(2,1)}, u32[]{:S(2)}) copy-start(bf16[768,768]{1,0:T(8,128)(2,1)} %param.41) | copy-start | bytes 3538948
  13.7 39.0 %copy-start.59 = (s32[1024,1]{0,1:T(1,128)}, s32[1024,1]{0,1:T(1,128)S(1)}, u32[]{:S(2)}) copy-start(s32[1024,1]{0,1:T(1,128)S(1)} %compare_select_fusion) | copy-start | bytes 12292
  47.8 4.9 copy-start.33
  47.8 76.1 %all-to-all-start.1 = ((bf16[8,256,768]{2,1,0:T(8,128)(2,1)}), bf16[8,256,768]{2,1,0:T(8,128)(2,1)}, u32[]{:S(2)}, u32[]{:S(2)}) async-start(bf16[8,256,768]{2,1,0:T(8,128)(2,1)} %broadcast_select_fusion), calls=%async_computation.1 | async-start | bytes 6291456 | tf_op jit(solution)/shard_map/all_to_all | solution.py:120
  52.4 388.1 %reduce-scatter.11.cloned.1.call-start = ((), (), s32[]{:S(2)}) async-start(), calls=%async_computation.11 | async-start | bytes 1769472 | tf_op jit(solution)/shard_map/reduce_scatter | solution.py:252
  123.9 7.9 copy-start.61
  123.9 7.9 copy-start.69
  144.2 5.5 copy-start.75
  153.9 5.4 copy-start.76
  163.6 4.1 copy-start.79
  193.4 4.1 copy-start.2
  193.4 4.1 copy-start.17
  193.4 4.1 copy-start.77
  197.5 39.9 %slice-start = ((s8[4718592]{0:T(1024)(128)(4,1)}), s8[4194304]{0:T(1024)(128)(4,1)S(1)}, s32[]{:S(2)}) async-start(s8[4718592]{0:T(1024)(128)(4,1)} %bitcast.281), calls=%async_computation.20 | async-start | bytes 8388608
  199.2 38.2 %copy-start.7 = (f32[1024,768]{1,0:T(8,128)}, f32[1024,768]{1,0:T(8,128)S(1)}, u32[]{:S(2)}) copy-start(f32[1024,768]{1,0:T(8,128)S(1)} %get-tuple-element.280) | copy-start | bytes 9437188
  199.3 81.5 %copy-start.36 = (f32[1024]{0:T(1024)}, f32[1024]{0:T(1024)S(1)}, u32[]{:S(2)}) copy-start(f32[1024]{0:T(1024)S(1)} %broadcast_multiply_fusion.1) | copy-start | bytes 12292
  201.9 78.9 %copy-start.38 = (f32[1024]{0:T(1024)}, f32[1024]{0:T(1024)S(1)}, u32[]{:S(2)}) copy-start(f32[1024]{0:T(1024)S(1)} %fusion.81) | copy-start | bytes 12292
  201.9 35.5 %slice-start.1 = ((s8[4718592]{0:T(1024)(128)(4,1)}), s8[524288]{0:T(1024)(128)(4,1)S(1)}, s32[]{:S(2)}) async-start(s8[4718592]{0:T(1024)(128)(4,1)} %bitcast.281), calls=%async_computation.21 | async-start | bytes 1048576
  201.9 35.6 %copy-start.78 = (f32[768]{0:T(1024)S(1)}, f32[768]{0:T(1024)}, u32[]{:S(2)}) copy-start(f32[768]{0:T(1024)} %param.48) | copy-start | bytes 9220
  237.4 5.5 copy-start.82
  249.6 19.6 %copy-start.57 = (f32[1024]{0:T(1024)}, f32[1024]{0:T(1024)S(1)}, u32[]{:S(2)}) copy-start(f32[1024]{0:T(1024)S(1)} %negate_multiply_fusion.3) | copy-start | bytes 12292
  269.2 11.6 %copy-start.8 = (f32[1024,768]{1,0:T(8,128)S(1)}, f32[1024,768]{1,0:T(8,128)}, u32[]{:S(2)}) copy-start(f32[1024,768]{1,0:T(8,128)} %copy-done.7) | copy-start | bytes 9437188
  287.1 6.9 copy-start.3
  287.1 6.9 copy-start.35
  287.1 6.9 copy-start.80
  301.6 7.3 copy-start.19
  309.0 7.3 copy-start.23
  328.9 7.3 copy-start.19
  336.3 7.3 copy-start.23
  358.8 3.6 copy-start.26
  374.9 73.1 %reduce-scatter.19.cloned.1.call-start = ((), (), s32[]{:S(2)}) async-start(), calls=%async_computation.15 | async-start | bytes 2654208 | tf_op jit(solution)/shard_map/reduce_scatter | solution.py:246
  380.2 139.9 %reduce-scatter.15.cloned.1.call-start = ((), (), s32[]{:S(2)}) async-start(), calls=%async_computation.13 | async-start | bytes 2654208 | tf_op jit(solution)/shard_map/reduce_scatter | solution.py:243
  385.0 181.0 %reduce-scatter.13.cloned.1.call-start = ((), (), s32[]{:S(2)}) async-start(), calls=%async_computation.12 | async-start | bytes 2654208 | tf_op jit(solution)/shard_map/reduce_scatter | solution.py:241
  389.9 4.4 copy-start.58
  389.9 213.9 %reduce-scatter.17.cloned.1.call-start = ((), (), s32[]{:S(2)}) async-start(), calls=%async_computation.14 | async-start | bytes 2654208 | tf_op jit(solution)/shard_map/reduce_scatter | solution.py:244
  394.2 310.6 %reduce-scatter.23.cloned.1.call-start = ((), (), s32[]{:S(2)}) async-start(), calls=%async_computation.17 | async-start | bytes 10616832 | tf_op jit(solution)/shard_map/reduce_scatter | solution.py:254
  404.9 400.0 %reduce-scatter.21.cloned.1.call-start = ((), (), s32[]{:S(2)}) async-start(), calls=%async_computation.16 | async-start | bytes 10616832 | tf_op jit(solution)/shard_map/reduce_scatter | solution.py:256
  430.4 4.7 copy-start.62
  430.4 175.1 %all-to-all-start.2 = ((bf16[8,256,768]{2,1,0:T(8,128)(2,1)}), bf16[8,256,768]{2,1,0:T(8,128)(2,1)}, u32[]{:S(2)}, u32[]{:S(2)}) async-start(bf16[8,256,768]{2,1,0:T(8,128)(2,1)} %bitcast.248), calls=%async_computation.2 | async-start | bytes 6291456 | tf_op jit(solution)/shard_map/all_to_all | solution.py:206
  435.0 170.5 %copy-start.56 = (pred[8,256]{1,0:T(8,128)(4,1)S(1)}, pred[8,256]{1,0:T(8,128)(4,1)}, u32[]{:S(2)}) copy-start(pred[8,256]{1,0:T(8,128)(4,1)} %copy-done.55) | copy-start | bytes 6148
  435.0 407.1 %reduce-scatter.25.cloned.1.call-start = ((), (), s32[]{:S(2)}) async-start(), calls=%async_computation.18 | async-start | bytes 442368
  440.4 566.6 %all-reduce.16.cloned.1.call-start = ((), (), s32[]{:S(2)}) async-start(), calls=%async_computation.19 | async-start | bytes 15532032 | tf_op jit(solution)/shard_map/psum | solution.py:302
  810.1 4.4 copy-start.63
  810.1 4.4 copy-start.64
  810.1 4.4 copy-start.67
  810.1 4.4 copy-start.68
  1007.0 10.4 %copy-start.34 = (bf16[384,768]{1,0:T(8,128)(2,1)S(1)}, bf16[384,768]{1,0:T(8,128)(2,1)}, u32[]{:S(2)}) copy-start(bf16[384,768]{1,0:T(8,128)(2,1)} %get-tuple-element.257) | copy-start | bytes 1769476
  1018.5 8.2 copy-start.1
  (60 other events, 120.2 us)
Sparse Core Ops, SparseCore 0:
  375.0 33.1 reduce-scatter.10
  410.5 37.4 reduce-scatter.18
  450.3 69.7 reduce-scatter.14
  522.3 43.6 reduce-scatter.12
  568.1 35.6 reduce-scatter.16
  606.0 98.7 reduce-scatter.22
  707.1 97.8 reduce-scatter.20
  807.2 29.2 reduce-scatter.24
  843.6 163.4 all-reduce.15
where the time goes:
time: 1040 us; the launch traced here: 1030 us
  waiting for transfers between devices  540 us (52%)
  matrix products  186 us (18%)
  other arithmetic  137 us (13%)
  local copies, waits for them, and re-layouts  95 us (9%)
  blocking collectives  48.7 us (5%)
  between operations  16.5 us (2%)
    psum x1, waiting for transfers between devices, local(): lax.psum(grad_word.astype(jnp.bfloat16), 'dp').astype(jnp.float32)  148 us
    reduce_scatter x1, waiting for transfers between devices, local(): lax.psum_scatter(grad_up, 'vocab', scatter_dimension=0, tiled=True)  98.1 us
    all_to_all x1, waiting for transfers between devices, local(): lax.all_to_all(found, 'vocab', split_axis=0, concat_axis=0, tiled=True)  71.1 us
    reduce_scatter x1, waiting for transfers between devices, local(): lax.psum_scatter(grad_key_weight, 'vocab', scatter_dimension=0, tiled=True)  70.5 us
    reduce_scatter x1, waiting for transfers between devices, local(): lax.psum_scatter(grad_down, 'vocab', scatter_dimension=0, tiled=True)  66.6 us
    dot_general x6, matrix products, matmul(): return jnp.dot(left, right, preferred_element_type=jnp.float32)  50.3 us
    reduce_scatter x1, waiting for transfers between devices, local(): lax.psum_scatter(grad_query_weight, 'vocab', scatter_dimension=0, tiled=T...  44.2 us
    dot_general x6, matrix products, matmul_tn(): lax.dot_general(left, right, (((0,), (0,)), ((), ())), preferred_element_...  40.9 us
  transfers between devices with their start and end apart: 11, of which 8 were waited for; matrix products, arithmetic and copies ran while one was open for 11% of the time, Pallas kernels for 0%

commit v1 on v0

--- a/solution.py
+++ b/solution.py
@@ -8,6 +8,12 @@
 HEAD = 64
 L = 512
 EPSILON = 1e-12
+
+
+def gather_and_add(shard, name):
+    parts = lax.all_gather(shard, name, axis=0, tiled=False)
+    total = parts.sum(axis=0)
+    return total
 
 
 def layer_norm(values, gain, bias):
@@ -299,7 +305,7 @@
         lax.psum(grad_up_bias.astype(jnp.bfloat16), "dp").astype(jnp.float32),
         lax.psum(grad_final_gain.astype(jnp.bfloat16), "dp").astype(jnp.float32),
         lax.psum(grad_final_bias.astype(jnp.bfloat16), "dp").astype(jnp.float32),
-        lax.psum(grad_word.astype(jnp.bfloat16), "dp").astype(jnp.float32),
+        gather_and_add(grad_word.astype(jnp.bfloat16), "dp").astype(jnp.float32),
     )
     return (
         encoded.reshape(seq_count, seq_len, width),

time: 1040 us -> 1170 us (1.12)
  waiting for transfers between devices: 540 us -> 653 us
    all_gather x0 -> x1, waiting for transfers between devices: none -> 209 us  [gather_and_add(): parts = lax.all_gather(shard, name, axis=0, tiled=False)]
    psum x1, waiting for transfers between devices: 148 us -> 17.6 us  [local(): lax.psum(grad_pos.astype(jnp.bfloat16), 'dp').astype(jnp.float32)]
    reduce_scatter x1, waiting for transfers between devices: 70.5 us -> 36.1 us  [local(): lax.psum_scatter(grad_key_weight, 'vocab', scatter_dimension=0, tiled=True)]
    reduce_scatter x1, waiting for transfers between devices: 66.6 us -> 99.2 us  [local(): lax.psum_scatter(grad_down, 'vocab', scatter_dimension=0, tiled=True)]
    reduce_scatter x1, waiting for transfers between devices: 44.2 us -> 71 us  [local(): lax.psum_scatter(grad_query_weight, 'vocab', scatter_dimension=0, tiled=T...]
    reduce_sum x0 -> x1, other arithmetic: none -> 15.9 us  [gather_and_add(): total = parts.sum(axis=0)]
  transfers between devices with their start and end apart: 11 -> 12, of which waited for: 8 -> 9; matrix products, arithmetic and copies ran while one was open for 11% -> 11% of each run, Pallas kernels for 0% -> 0%
where the time goes in v1:
time: 1170 us; the launch traced here: 1160 us
  waiting for transfers between devices  653 us (56%)
  matrix products  188 us (16%)
  other arithmetic  147 us (13%)
  local copies, waits for them, and re-layouts  97 us (8%)
  blocking collectives  48.3 us (4%)
  between operations  16.8 us (1%)
    all_gather x1, waiting for transfers between devices, gather_and_add(): parts = lax.all_gather(shard, name, axis=0, tiled=False)  209 us
    reduce_scatter x1, waiting for transfers between devices, local(): lax.psum_scatter(grad_down, 'vocab', scatter_dimension=0, tiled=True)  99.2 us
    reduce_scatter x1, waiting for transfers between devices, local(): lax.psum_scatter(grad_up, 'vocab', scatter_dimension=0, tiled=True)  98.6 us
    all_to_all x1, waiting for transfers between devices, local(): lax.all_to_all(found, 'vocab', split_axis=0, concat_axis=0, tiled=True)  71.1 us
    reduce_scatter x1, waiting for transfers between devices, local(): lax.psum_scatter(grad_query_weight, 'vocab', scatter_dimension=0, tiled=T...  71 us
    dot_general x6, matrix products, matmul(): return jnp.dot(left, right, preferred_element_type=jnp.float32)  50.4 us
    reduce_scatter x1, waiting for transfers between devices, local(): lax.psum_scatter(grad_value_weight, 'vocab', scatter_dimension=0, tiled=T...  44.4 us
    dot_general x6, matrix products, matmul_tn(): lax.dot_general(left, right, (((0,), (0,)), ((), ())), preferred_element_...  40.9 us
  transfers between devices with their start and end apart: 12, of which 9 were waited for; matrix products, arithmetic and copies ran while one was open for 11% of the time, Pallas kernels for 0%

profile of v1, /device:TPU:0, one launch (start us, length us, event | category | flops | bytes accessed | tf_op | source)
XLA Modules:
  0.0 1160.7 jit_solution(6130373292369219467)
XLA Ops:
  13.8 4.3 scatter_custom_fusion
  18.1 11.7 %all_to_all.19 = s32[8,1,256]{2,1,0:T(1,128)S(1)} all-to-all(s32[8,1,256]{2,1,0:T(1,128)S(1)} %bitcast.272), channel_id=1, replica_groups=mesh['dp'=4,'vocab'=8] {'vocab'}, dimensions={0} | all-to-all | bytes 16384 | tf_op jit(solution)/shard_map/all_to_all | solution.py:122
  30.4 13.5 %gather_fusion = bf16[2048,768]{1,0:T(8,128)(2,1)} fusion(bf16[3840,768]{1,0:T(8,128)(2,1)} %param.31, s32[2048]{0:T(1024)S(1)} %broadcast_clamp_fusion), kind=kCustom, calls=%fused_computation | custom fusion | bytes 6299648 | tf_op jit(solution)/shard_map/gather | solution.py:124
  47.8 4.6 all-to-all-start.1
  52.8 71.1 %all-to-all-done.1 = bf16[8,256,768]{2,1,0:T(8,128)(2,1)} async-done(((bf16[8,256,768]{2,1,0:T(8,128)(2,1)}), bf16[8,256,768]{2,1,0:T(8,128)(2,1)}, u32[]{:S(2)}, u32[]{:S(2)}) %all-to-all-start.1) | async-done | bytes 3145760 | tf_op jit(solution)/shard_map/all_to_all | solution.py:126
  123.9 7.9 gather_fusion.1
  170.5 25.6 %while.26 = (s32[]{:T(128)}, bf16[2,512,12,64]{1,3,2,0:T(8,128)(2,1)}, f32[2,12,512,1]{2,1,3,0:T(8,128)}, bf16[2,512,12,64]{1,3,2,0:T(8,128)(2,1)}, s32[2]{0:T(1...) while((s32[]{:T(128)}, ...), condition=%wide.region_9.10_spmd, body=%wide.region_6.9_spmd.sunk | while | flops 843442688 | bytes 47411840 | solution.py:150
  171.9 4.1 fusion.155
  179.2 4.1 fusion.157
  184.6 4.1 fusion.155
  191.9 4.2 fusion.157
  204.6 35.5 %multiply_convert_fusion.1 = (bf16[1024,3072]{1,0:T(8,128)(2,1)S(1)}, f32[1024,3072]{1,0:T(8,128)}, f32[1024,3072]{1,0:T(8,128)}) fusion(f32[3072]{0:T(1024)S(1)} %copy-done.77, bf16[768,3072]{1,0:T(8,128)(2,1)S(1)} %bitcast.284, f32[1024,768]{1,0:T(8,128)S(1)} %get-tuple-element.296, f32[768]{0:T(1024)S(1)} %copy-done.51, f32[768]{0:T(1024)S(1)} %copy-done.45, ...), kind=kOutput, calls=%fused_computation.64 | convolution fusion | flops 5043388416 | bytes 39348224 | tf_op jit(solution)/shard_map/dot_general | solution.py:26
  240.2 5.4 fusion.98
  252.3 19.7 %fusion.100 = (f32[3072]{0:T(1024)}, bf16[1024,3072]{1,0:T(8,128)(2,1)}) fusion(f32[1024,3072]{1,0:T(8,128)} %get-tuple-element.281, bf16[3072,768]{1,0:T(8,128)(2,1)} %param.47, f32[1024,768]{1,0:T(8,128)} %get-tuple-element.279, f32[1024]{0:T(1024)S(1)} %negate_multiply_fusion.3, f32[1024,3072]{1,0:T(8,128)} %get-tuple-element.297, f32[3072]{0:T(1024)S(1)} %copy-done.77), kind=kOutput, calls=%fused_computation.197 | convolution fusion | flops 4883739648 | bytes 39350272 | tf_op jit(solution)/shard_map/dot_general | solution.py:36
  272.0 11.6 multiply_reduce_fusion.1
  289.9 4.0 reshape.389
  296.8 56.0 %while.27 = (s32[]{:T(128)}, f32[2,512,12,64]{1,3,2,0:T(8,128)}, bf16[2,512,12,64]{1,3,2,0:T(8,128)(2,1)}, f32[2,512,12,64]{1,3,2,0:T(8,128)}, bf16[2,512,12,64]...) while((s32[]{:T(128)}, f32[2,512,12,64]{1,3,2,0:T(8,128)}, ...), condition=%wide.region_20.21_spmd, body=%wide.region_18.20_spmd.sunk | while | flops 2061232640 | bytes 161414480 | solution.py:178
  301.5 7.3 multiply_reduce_fusion.9
  308.8 7.4 multiply_convert_fusion.3
  320.8 3.9 bitcast_dynamic-update-slice_fusion.11
  329.2 7.3 multiply_reduce_fusion.9
  336.5 7.4 multiply_convert_fusion.3
  352.8 5.5 fusion.94
  378.8 5.2 fusion.86
  384.1 4.8 fusion.103
  388.9 4.3 fusion.105
  393.3 4.7 fusion.104
  398.1 10.7 fusion.85
  409.5 11.2 fusion.60
  420.8 8.7 scatter_custom_fusion.1
  429.4 4.8 convert_element_type.254
  434.2 4.6 all-to-all-start.2
  438.9 5.3 convolution_bitcast_fusion
  445.8 6.0 reduce-scatter.19.cloned.1.call-done
  453.5 71.0 %reduce-scatter.13.cloned.1.call-done = f32[96,768]{1,0:T(8,128)} async-done(((f32[768,768]{1,0:T(8,128)}), f32[96,768]{1,0:T(8,128)}) %reduce-scatter.13.cloned.1.call-update) | async-done | bytes 294928 | tf_op jit(solution)/shard_map/reduce_scatter | solution.py:247
  526.1 44.4 %reduce-scatter.17.cloned.1.call-done = f32[96,768]{1,0:T(8,128)} async-done(((f32[768,768]{1,0:T(8,128)}), f32[96,768]{1,0:T(8,128)}) %reduce-scatter.17.cloned.1.call-update) | async-done | bytes 294928 | tf_op jit(solution)/shard_map/reduce_scatter | solution.py:250
  572.1 36.1 %reduce-scatter.15.cloned.1.call-done = f32[96,768]{1,0:T(8,128)} async-done(((f32[768,768]{1,0:T(8,128)}), f32[96,768]{1,0:T(8,128)}) %reduce-scatter.15.cloned.1.call-update) | async-done | bytes 294928 | tf_op jit(solution)/shard_map/reduce_scatter | solution.py:249
  609.9 99.2 %reduce-scatter.23.cloned.1.call-done = f32[384,768]{1,0:T(8,128)} async-done(((f32[3072,768]{1,0:T(8,128)}), f32[384,768]{1,0:T(8,128)}) %reduce-scatter.23.cloned.1.call-update) | async-done | bytes 1179664 | tf_op jit(solution)/shard_map/reduce_scatter | solution.py:260
  711.2 98.6 %reduce-scatter.21.cloned.1.call-done = f32[96,3072]{1,0:T(8,128)} async-done(((f32[768,3072]{1,0:T(8,128)}), f32[96,3072]{1,0:T(8,128)}) %reduce-scatter.21.cloned.1.call-update) | async-done | bytes 1179664 | tf_op jit(solution)/shard_map/reduce_scatter | solution.py:262
  812.1 4.7 convert_select_fusion
  816.8 20.3 %scatter_custom_fusion.2 = f32[3840,768]{1,0:T(8,128)} fusion(s32[2048]{0:T(1024)} %bitcast.271, f32[2048,768]{1,0:T(8,128)} %bitcast.250, f32[]{:T(128)} %constant.48.clone.1), kind=kCustom, calls=%fused_computation.79 | custom fusion | flops 1572864 | bytes 11796992 | tf_op jit(solution)/shard_map/scatter-add | solution.py:224
  837.1 7.4 convert_element_type.257
  850.7 26.4 %all-reduce.11 = (bf16[768]{0:T(1024)(128)(2,1)S(1)}, bf16[768]{0:T(1024)(128)(2,1)S(1)}, bf16[768]{0:T(1024)(128)(2,1)S(1)}, bf16[768]{0:T(1024)(128)(2,1)S(1)}...) all-reduce(f32[768]{0:T(1024)S(1)} %get-tuple-element.207, ...), channel_id=5, replica_groups=mesh['dp'=4,'vocab'=8] {'vocab'}, use_global_device_ids=true, to_apply=%region_32.33.clone | all-reduce | flops 10752 | bytes 64512
  878.8 10.1 all-reduce.12
  895.2 17.6 %all-reduce.16.cloned.1.call-done = (bf16[64,768]{1,0:T(8,128)(2,1)}, bf16[96,768]{1,0:T(8,128)(2,1)}, bf16[96,768]{1,0:T(8,128)(2,1)}, bf16[96,768]{1,0:T(8,128...) async-done(((bf16[64,768]{1,0:T(8,128)(2,1)}, bf16[96,768]{1,0:T(8,128)(2,1)}, bf16[96,768]{1,0:T(8,128)(2,1)}, ...) | async-done | bytes 1867792 | tf_op jit(solution)/shard_map/psum | solution.py:300
  920.9 208.6 %all-gather.3.cloned.1.call-done = bf16[15360,768]{1,0:T(8,128)(2,1)} async-done(((bf16[3840,768]{1,0:T(8,128)(2,1)}), bf16[15360,768]{1,0:T(8,128)(2,1)}) %all-gather.3.cloned.1.call-update) | async-done | bytes 23592976 | tf_op jit(solution)/shard_map/all_gather | solution.py:14
  1129.5 15.9 %reduce_sum.288 = bf16[3840,768]{1,0:T(8,128)(2,1)} reduce(bf16[4,3840,768]{2,1,0:T(8,128)(2,1)} %bitcast.247, bf16[]{:T(256)} %constant.47.clone.1), dimensions={0}, to_apply=%region_25.26 | reduce | flops 8847360 | bytes 29491202 | tf_op jit(solution)/shard_map/reduce_sum | solution.py:15
  1145.4 8.2 convert_element_type.258
  (368 shorter events, 159.3 us)
Async XLA Ops:
  7.2 193.0 %copy-start = (bf16[768,768]{1,0:T(8,128)(2,1)S(1)}, bf16[768,768]{1,0:T(8,128)(2,1)}, u32[]{:S(2)}) copy-start(bf16[768,768]{1,0:T(8,128)(2,1)} %param.41) | copy-start | bytes 3538948
  13.7 39.0 %copy-start.62 = (s32[1024,1]{0,1:T(1,128)}, s32[1024,1]{0,1:T(1,128)S(1)}, u32[]{:S(2)}) copy-start(s32[1024,1]{0,1:T(1,128)S(1)} %compare_select_fusion) | copy-start | bytes 12292
  47.8 4.9 copy-start.32
  47.8 76.1 %all-to-all-start.1 = ((bf16[8,256,768]{2,1,0:T(8,128)(2,1)}), bf16[8,256,768]{2,1,0:T(8,128)(2,1)}, u32[]{:S(2)}, u32[]{:S(2)}) async-start(bf16[8,256,768]{2,1,0:T(8,128)(2,1)} %broadcast_select_fusion), calls=%async_computation.1 | async-start | bytes 6291456 | tf_op jit(solution)/shard_map/all_to_all | solution.py:126
  52.3 391.9 %reduce-scatter.11.cloned.1.call-start = ((), (), s32[]{:S(2)}) async-start(), calls=%async_computation.11 | async-start | bytes 1769472 | tf_op jit(solution)/shard_map/reduce_scatter | solution.py:258
  123.9 7.9 copy-start.64
  123.9 7.9 copy-start.72
  144.1 5.5 copy-start.79
  163.7 6.7 copy-start.82
  200.2 39.9 %slice-start = ((s8[4718592]{0:T(1024)(128)(4,1)}), s8[4194304]{0:T(1024)(128)(4,1)S(1)}, s32[]{:S(2)}) async-start(s8[4718592]{0:T(1024)(128)(4,1)} %bitcast.281), calls=%async_computation.21 | async-start | bytes 8388608
  201.9 38.2 %copy-start.7 = (f32[1024,768]{1,0:T(8,128)}, f32[1024,768]{1,0:T(8,128)S(1)}, u32[]{:S(2)}) copy-start(f32[1024,768]{1,0:T(8,128)S(1)} %get-tuple-element.296) | copy-start | bytes 9437188
  202.0 81.6 %copy-start.34 = (f32[1024]{0:T(1024)}, f32[1024]{0:T(1024)S(1)}, u32[]{:S(2)}) copy-start(f32[1024]{0:T(1024)S(1)} %broadcast_multiply_fusion.1) | copy-start | bytes 12292
  204.6 79.0 %copy-start.36 = (f32[1024]{0:T(1024)}, f32[1024]{0:T(1024)S(1)}, u32[]{:S(2)}) copy-start(f32[1024]{0:T(1024)S(1)} %fusion.81) | copy-start | bytes 12292
  204.6 35.5 %slice-start.1 = ((s8[4718592]{0:T(1024)(128)(4,1)}), s8[524288]{0:T(1024)(128)(4,1)S(1)}, s32[]{:S(2)}) async-start(s8[4718592]{0:T(1024)(128)(4,1)} %bitcast.281), calls=%async_computation.22 | async-start | bytes 1048576
  204.6 35.5 %copy-start.81 = (f32[768]{0:T(1024)S(1)}, f32[768]{0:T(1024)}, u32[]{:S(2)}) copy-start(f32[768]{0:T(1024)} %param.48) | copy-start | bytes 9220
  240.1 5.5 copy-start.85
  252.3 19.7 %copy-start.60 = (f32[1024]{0:T(1024)}, f32[1024]{0:T(1024)S(1)}, u32[]{:S(2)}) copy-start(f32[1024]{0:T(1024)S(1)} %negate_multiply_fusion.3) | copy-start | bytes 12292
  272.0 11.6 copy-start.8
  289.9 6.9 copy-start.3
  289.9 6.9 copy-start.33
  289.9 6.9 copy-start.83
  297.1 4.4 copy-start.12
  297.1 4.4 copy-start.13
  308.8 7.4 copy-start.4
  308.8 7.4 copy-start.19
  324.8 4.4 copy-start.12
  324.8 4.4 copy-start.13
  336.5 7.4 copy-start.4
  336.5 7.4 copy-start.19
  378.7 73.1 %reduce-scatter.19.cloned.1.call-start = ((), (), s32[]{:S(2)}) async-start(), calls=%async_computation.15 | async-start | bytes 2654208 | tf_op jit(solution)/shard_map/reduce_scatter | solution.py:252
  384.0 140.4 %reduce-scatter.13.cloned.1.call-start = ((), (), s32[]{:S(2)}) async-start(), calls=%async_computation.12 | async-start | bytes 2654208 | tf_op jit(solution)/shard_map/reduce_scatter | solution.py:247
  388.9 181.6 %reduce-scatter.17.cloned.1.call-start = ((), (), s32[]{:S(2)}) async-start(), calls=%async_computation.14 | async-start | bytes 2654208 | tf_op jit(solution)/shard_map/reduce_scatter | solution.py:250
  393.3 4.9 copy-start.61
  393.3 214.9 %reduce-scatter.15.cloned.1.call-start = ((), (), s32[]{:S(2)}) async-start(), calls=%async_computation.13 | async-start | bytes 2654208 | tf_op jit(solution)/shard_map/reduce_scatter | solution.py:249
  398.1 311.0 %reduce-scatter.23.cloned.1.call-start = ((), (), s32[]{:S(2)}) async-start(), calls=%async_computation.17 | async-start | bytes 10616832 | tf_op jit(solution)/shard_map/reduce_scatter | solution.py:260
  408.8 401.0 %reduce-scatter.21.cloned.1.call-start = ((), (), s32[]{:S(2)}) async-start(), calls=%async_computation.16 | async-start | bytes 10616832 | tf_op jit(solution)/shard_map/reduce_scatter | solution.py:262
  434.2 4.7 copy-start.65
  434.2 377.9 %all-to-all-start.2 = ((bf16[8,256,768]{2,1,0:T(8,128)(2,1)}), bf16[8,256,768]{2,1,0:T(8,128)(2,1)}, u32[]{:S(2)}, u32[]{:S(2)}) async-start(bf16[8,256,768]{2,1,0:T(8,128)(2,1)} %bitcast.248), calls=%async_computation.2 | async-start | bytes 6291456 | tf_op jit(solution)/shard_map/all_to_all | solution.py:212
  438.8 439.1 %reduce-scatter.25.cloned.1.call-start = ((), (), s32[]{:S(2)}) async-start(), calls=%async_computation.19 | async-start | bytes 442368
  444.2 468.6 %all-reduce.16.cloned.1.call-start = ((), (), s32[]{:S(2)}) async-start(), calls=%async_computation.20 | async-start | bytes 3735552 | tf_op jit(solution)/shard_map/psum | solution.py:300
  526.1 286.0 %copy-start.59 = (pred[8,256]{1,0:T(8,128)(4,1)S(1)}, pred[8,256]{1,0:T(8,128)(4,1)}, u32[]{:S(2)}) copy-start(pred[8,256]{1,0:T(8,128)(4,1)} %copy-done.58) | copy-start | bytes 6148
  812.0 317.4 %all-gather.3.cloned.1.call-start = ((), (), s32[]{:S(2)}) async-start(), calls=%async_computation.18 | async-start | bytes 29491200 | tf_op jit(solution)/shard_map/all_gather | solution.py:14
  912.8 4.4 copy-start.41
  912.8 5.1 copy-start.40
  912.8 5.9 copy-start.39
  912.8 6.6 copy-start.38
  912.8 7.4 copy-start.44
  1145.4 8.2 copy-start.1
  (62 other events, 130.0 us)
Sparse Core Ops, SparseCore 0:
  378.8 33.1 reduce-scatter.10
  414.3 37.4 reduce-scatter.18
  454.1 70.2 reduce-scatter.12
  526.6 43.8 reduce-scatter.16
  572.7 35.5 reduce-scatter.14
  610.4 98.6 reduce-scatter.22
  712.0 97.8 reduce-scatter.20
  812.1 28.9 reduce-scatter.24
  847.3 65.4 all-reduce.15
  914.7 214.7 all-gather.2
